TPU v7x, 512 devices: a whole 4x4x16 slice. The times are simulated.
512 devices in a mesh: dp: 16 (over y, x), seq: 32 (over z, core).
Axes of the slice: x: 4, y: 4, z: 16, core: 2. Of those that a mesh axis runs over, the one named last changes fastest.
Arguments:
- tokens: bfloat16 [16, 8192, 4096], P('dp', 'seq'), may hold values from -6 to 6
- w_qkv: bfloat16 [4096, 768], P('dp'), may hold values from -0.09375 to 0.09375
- norm_gain: float32 [256], replicated, may hold values from 0.1 to 1.9
- w_out: bfloat16 [256, 4096], P(None, 'dp'), may hold values from -0.375 to 0.375
Outputs:
- mixed: bfloat16 [16, 8192, 4096], P('dp', 'seq')
All inputs are finite; a program needn't handle non-finite values.
Results may differ from a plain program's by a relative error of at most 0.015.
Values may be sent and summed in bfloat16 or wider, within the bound.
A program may use at most 64 MiB of HBM per device.

v0:
```python
import jax
import jax.numpy as jnp
from jax import lax
from jax.sharding import PartitionSpec as P

HEAD = 128


def shards(tokens, w_qkv, norm_gain, w_out):
    inputs = tokens[0]
    tok_rows = inputs.shape[0]
    width3 = w_qkv.shape[1]
    feat = width3 // 3
    heads = norm_gain.shape[0] // HEAD
    proj = jnp.dot(
        inputs, lax.all_gather(w_qkv, "dp", axis=0, tiled=True), preferred_element_type=jnp.float32
    )
    query = jax.nn.silu(proj[:, :feat]).astype(jnp.bfloat16).reshape(tok_rows, heads, HEAD)
    keys = jax.nn.silu(proj[:, feat : 2 * feat]).astype(jnp.bfloat16).reshape(tok_rows, heads, HEAD)
    values = proj[:, 2 * feat :].astype(jnp.bfloat16).reshape(tok_rows, heads, HEAD)
    state = jnp.einsum("thA,thB->hAB", keys, values, preferred_element_type=jnp.float32)
    every_state = lax.all_gather(
        state[None].astype(jnp.bfloat16), "seq", axis=0, tiled=True
    ).astype(jnp.float32)
    blocks = every_state.shape[0]
    weights = (jnp.arange(blocks) < lax.axis_index("seq")).astype(jnp.float32)
    prefix = jnp.einsum("n,nhab->hab", weights, every_state, precision=lax.Precision.HIGHEST)
    prefix = prefix.astype(jnp.bfloat16)
    inter = jnp.einsum("thA,hAB->thB", query, prefix, preferred_element_type=jnp.float32)
    scores = jnp.einsum("thA,shA->hts", query, keys, preferred_element_type=jnp.float32)
    rows = jnp.arange(tok_rows)
    causal = rows[:, None] >= rows[None, :]
    scores = jnp.where(causal[None], scores, 0.0).astype(jnp.bfloat16)
    intra = jnp.einsum("hts,shB->thB", scores, values, preferred_element_type=jnp.float32)
    attended = inter + intra
    meansq = jnp.mean(attended * attended, axis=-1, keepdims=True)
    normed = attended * lax.rsqrt(meansq + 1e-06) * norm_gain.reshape(heads, HEAD)
    normed = normed.astype(jnp.bfloat16).reshape(tok_rows, heads * HEAD)
    mixed = jnp.dot(
        normed, lax.all_gather(w_out, "dp", axis=1, tiled=True), preferred_element_type=jnp.float32
    )
    return mixed.astype(jnp.bfloat16)[None]


def solution(mesh):
    return jax.shard_map(
        shards,
        mesh=mesh,
        in_specs=(P("dp", "seq", None), P("dp", None), P(), P(None, "dp")),
        out_specs=P("dp", "seq", None),
        check_vma=False,
    )
```

profile of v0, /device:TPU:1, one launch (start us, length us, event | category | flops | bytes accessed | tf_op | source)
XLA Modules:
  0.0 242.1 jit_solution(8243178207157146970)
XLA Ops:
  6.5 0.0 copy-start
  6.5 0.0 all-gather.5.cloned.1.call-start
  6.5 0.7 all-gather.5.cloned.1.call-update
  7.3 0.0 all-gather.9.cloned.1.call-start
  7.3 85.1 %all-gather.5.cloned.1.call-done = bf16[4096,768]{1,0:T(8,128)(2,1)} async-done(((bf16[256,768]{1,0:T(8,128)(2,1)}), bf16[4096,768]{1,0:T(8,128)(2,1)}) %all-gather.5.cloned.1.call-update) | async-done | bytes 6291472 | tf_op jit(solution)/shard_map/all_gather | solution.py:16
  92.4 0.0 copy-done
  92.4 4.6 %fusion.1 = f32[256,768]{1,0:T(8,128)S(1)} fusion(bf16[4096,768]{1,0:T(8,128)(2,1)} %all-gather.5.cloned.1.call-done, bf16[1,256,4096]{2,1,0:T(8,128)(2,1)S(1)} %copy-done), kind=kOutput, calls=%fused_computation.2 | convolution fusion | flops 1610612736 | bytes 9175040 | tf_op jit(solution)/shard_map/dot_general | solution.py:15
  96.9 0.1 fusion.13
  97.1 0.1 copy.16
  97.2 0.1 copy.17
  97.3 0.8 convolution_convert_fusion.1
  98.2 0.0 all-gather.9.cloned.1.call-update
  98.2 0.0 copy-start.1
  98.2 0.0 all-gather.7.cloned.1.call-start
  98.2 0.7 all-gather.7.cloned.1.call-update
  99.0 0.4 fusion.6
  99.3 71.0 %all-gather.9.cloned.1.call-done = bf16[64,128,128]{2,1,0:T(8,128)(2,1)} async-done(((bf16[2,128,128]{2,1,0:T(8,128)(2,1)}), bf16[64,128,128]{2,1,0:T(8,128)(2,1)}) %all-gather.9.cloned.1.call-update) | async-done | bytes 2097168 | tf_op jit(solution)/shard_map/all_gather | solution.py:22
  170.3 2.9 %fusion.3 = bf16[1,2,128,128]{3,0,2,1:T(2,128)(2,1)S(1)} fusion(bf16[32,2,128,128]{3,2,1,0:T(8,128)(2,1)} %bitcast.39, s32[]{:T(128)S(6)} %axis_index.12), kind=kOutput, calls=%fused_computation.4 | convolution fusion | flops 2097184 | bytes 2162692 | tf_op jit(solution)/shard_map/n,nhab->hab/dot_general | solution.py:27
  173.2 0.1 copy.15
  173.3 0.2 multiply_reduce_fusion
  173.5 0.0 copy-done.1
  173.6 0.1 multiply_convert_fusion
  173.7 58.3 %all-gather.7.cloned.1.call-done = bf16[256,4096]{1,0:T(8,128)(2,1)} async-done(((bf16[256,256]{1,0:T(8,128)(2,1)}), bf16[256,4096]{1,0:T(8,128)(2,1)}) %all-gather.7.cloned.1.call-update) | async-done | bytes 2097168 | tf_op jit(solution)/shard_map/all_gather | solution.py:40
  231.9 3.6 %fusion = bf16[1,256,4096]{2,1,0:T(8,128)(2,1)} fusion(bf16[256,256]{0,1:T(8,128)(2,1)S(1)} %bitcast.40, bf16[256,4096]{1,0:T(8,128)(2,1)} %all-gather.7.cloned.1.call-done), kind=kOutput, calls=%fused_computation.1 | convolution fusion | flops 537919488 | bytes 4325376 | tf_op jit(solution)/shard_map/dot_general | solution.py:39
  (3 shorter events, 0.0 us)
Async XLA Ops:
  6.5 85.8 %copy-start = (bf16[1,256,4096]{2,1,0:T(8,128)(2,1)S(1)}, bf16[1,256,4096]{2,1,0:T(8,128)(2,1)}, u32[]{:S(2)}) copy-start(bf16[1,256,4096]{2,1,0:T(8,128)(2,1)} %param.4) | copy-start | bytes 6291460
  6.5 85.8 %all-gather.5.cloned.1.call-start = ((), (), s32[]{:S(2)}) async-start(), calls=%async_computation | async-start | bytes 6684672 | tf_op jit(solution)/shard_map/all_gather | solution.py:16
  7.3 163.1 %all-gather.9.cloned.1.call-start = ((), (), s32[]{:S(2)}) async-start(), calls=%async_computation.2 | async-start | bytes 2162688 | tf_op jit(solution)/shard_map/all_gather | solution.py:22
  98.2 75.4 %copy-start.1 = (f32[256]{0:T(256)S(1)}, f32[256]{0:T(256)}, u32[]{:S(2)}) copy-start(f32[256]{0:T(256)} %param.6) | copy-start | bytes 3076
  98.2 133.7 %all-gather.7.cloned.1.call-start = ((), (), s32[]{:S(2)}) async-start(), calls=%async_computation.1 | async-start | bytes 2228224 | tf_op jit(solution)/shard_map/all_gather | solution.py:40
Sparse Core Ops, SparseCore 0:
  10.4 81.9 all-gather.4
  98.3 71.9 all-gather.8
  173.3 58.5 all-gather.6
where the time goes:
time: 242 us
  waiting for transfers between devices  216 us (89%)
  between operations  13.2 us (5%)
  matrix products  12.4 us (5%)
    all_gather x1, waiting for transfers between devices, shards(): lax.all_gather(w_qkv, 'dp', axis=0, tiled=True)  85.1 us
    all_gather x1, waiting for transfers between devices, shards(): lax.all_gather(state[None].astype(jnp.bfloat16), 'seq', axis=0, tiled=True)  71 us
    all_gather x1, waiting for transfers between devices, shards(): lax.all_gather(w_out, 'dp', axis=1, tiled=True)  58.3 us
  transfers between devices with their start and end apart: 3, of which 3 were waited for; matrix products, arithmetic and copies ran while one was open for 2% of the time, Pallas kernels for 0%

commit v1 on v0

--- a/solution.py
+++ b/solution.py
@@ -19,9 +19,11 @@
     keys = jax.nn.silu(proj[:, feat : 2 * feat]).astype(jnp.bfloat16).reshape(tok_rows, heads, HEAD)
     values = proj[:, 2 * feat :].astype(jnp.bfloat16).reshape(tok_rows, heads, HEAD)
     state = jnp.einsum("thA,thB->hAB", keys, values, preferred_element_type=jnp.float32)
-    every_state = lax.all_gather(
-        state[None].astype(jnp.bfloat16), "seq", axis=0, tiled=True
-    ).astype(jnp.float32)
+    refer_cubes = lambda view: jnp.concatenate(
+        lax.all_to_all(jnp.stack([view for _ in range(lax.psum(1, "seq"))], axis=0), "seq", 0, 0),
+        axis=0,
+    )
+    every_state = refer_cubes(state[None].astype(jnp.bfloat16)).astype(jnp.float32)
     blocks = every_state.shape[0]
     weights = (jnp.arange(blocks) < lax.axis_index("seq")).astype(jnp.float32)
     prefix = jnp.einsum("n,nhab->hab", weights, every_state, precision=lax.Precision.HIGHEST)

time: 242 us -> 225 us (0.930)
  waiting for transfers between devices: 216 us -> 184 us
  starting transfers between devices: 0.08 us -> 13.1 us
    all_to_all x0 -> x1, waiting for transfers between devices: none -> 97.5 us  [shards(): lax.all_to_all(jnp.stack([view for _ in range(lax.psum(1, 'seq'))], axis=...]
    all_gather x1 -> x0, waiting for transfers between devices: 71 us -> none  [shards(): lax.all_gather(state[None].astype(jnp.bfloat16), 'seq', axis=0, tiled=True)]
    all_gather x1, waiting for transfers between devices: 58.3 us -> 0.02 us  [shards(): lax.all_gather(w_out, 'dp', axis=1, tiled=True)]
    all_to_all x0 -> x1, starting transfers between devices: none -> 13.1 us  [shards(): lax.all_to_all(jnp.stack([view for _ in range(lax.psum(1, 'seq'))], axis=...]
  transfers between devices with their start and end apart: 3 -> 3, of which waited for: 3 -> 2; matrix products, arithmetic and copies ran while one was open for 2% -> 2% of each run, Pallas kernels for 0% -> 0%
where the time goes in v1:
time: 225 us
  waiting for transfers between devices  184 us (82%)
  between operations  13.5 us (6%)
  starting transfers between devices  13.1 us (6%)
  matrix products  11.8 us (5%)
    all_to_all x1, waiting for transfers between devices, shards(): lax.all_to_all(jnp.stack([view for _ in range(lax.psum(1, 'seq'))], axis=...  97.5 us
    all_gather x1, waiting for transfers between devices, shards(): lax.all_gather(w_qkv, 'dp', axis=0, tiled=True)  85.1 us
    all_to_all x1, starting transfers between devices, shards(): lax.all_to_all(jnp.stack([view for _ in range(lax.psum(1, 'seq'))], axis=...  13.1 us
    dot_general x1, matrix products, shards(): jnp.dot(inputs, lax.all_gather(w_qkv, 'dp', axis=0, tiled=True), preferre...  4.56 us
  transfers between devices with their start and end apart: 3, of which 2 were waited for; matrix products, arithmetic and copies ran while one was open for 2% of the time, Pallas kernels for 0%

profile of v1, /device:TPU:1, one launch (start us, length us, event | category | flops | bytes accessed | tf_op | source)
XLA Modules:
  0.0 224.9 jit_solution(2538164592610223415)
XLA Ops:
  6.5 0.0 copy-start
  6.5 0.0 all-gather.3.cloned.1.call-start
  6.5 0.7 all-gather.3.cloned.1.call-update
  7.3 85.1 %all-gather.3.cloned.1.call-done = bf16[4096,768]{1,0:T(8,128)(2,1)} async-done(((bf16[256,768]{1,0:T(8,128)(2,1)}), bf16[4096,768]{1,0:T(8,128)(2,1)}) %all-gather.3.cloned.1.call-update) | async-done | bytes 6291472 | tf_op jit(solution)/shard_map/all_gather | solution.py:16
  92.4 0.0 copy-done
  92.4 4.6 %fusion.1 = f32[256,768]{1,0:T(8,128)S(1)} fusion(bf16[4096,768]{1,0:T(8,128)(2,1)} %all-gather.3.cloned.1.call-done, bf16[1,256,4096]{2,1,0:T(8,128)(2,1)S(1)} %copy-done), kind=kOutput, calls=%fused_computation.2 | convolution fusion | flops 1610612736 | bytes 9175040 | tf_op jit(solution)/shard_map/dot_general | solution.py:15
  96.9 0.1 fusion.13
  97.1 0.1 copy.12
  97.2 0.1 copy.13
  97.3 0.2 convolution_convert_fusion.1
  97.5 1.8 stack.2
  99.4 13.1 %all-to-all-start = ((bf16[32,1,2,128,128]{4,3,2,1,0:T(8,128)(2,1)}), bf16[32,1,2,128,128]{4,3,2,1,0:T(8,128)(2,1)}, u32[]{:S(2)}, u32[]{:S(2)}) async-start(bf16[32,1,2,128,128]{4,3,2,1,0:T(8,128)(2,1)} %stack.2), calls=%async_computation | async-start | bytes 4194304 | tf_op jit(solution)/shard_map/all_to_all | solution.py:23
  112.4 0.0 copy-start.1
  112.4 0.0 all-gather.5.cloned.1.call-start
  112.5 0.7 all-gather.5.cloned.1.call-update
  113.2 0.4 fusion.6
  113.6 97.5 %all-to-all-done = bf16[32,1,2,128,128]{4,3,2,1,0:T(8,128)(2,1)} async-done(((bf16[32,1,2,128,128]{4,3,2,1,0:T(8,128)(2,1)}), bf16[32,1,2,128,128]{4,3,2,1,0:T(8,128)(2,1)}, u32[]{:S(2)}, u32[]{:S(2)}) %all-to-all-start) | async-done | bytes 2097184 | tf_op jit(solution)/shard_map/all_to_all | solution.py:23
  211.1 2.9 %fusion.3 = bf16[1,2,128,128]{3,0,2,1:T(2,128)(2,1)S(1)} fusion(bf16[32,2,128,128]{3,2,1,0:T(8,128)(2,1)} %bitcast.4, s32[]{:T(128)S(6)} %axis_index.12), kind=kOutput, calls=%fused_computation.4 | convolution fusion | flops 2097184 | bytes 2162692 | tf_op jit(solution)/shard_map/n,nhab->hab/dot_general | solution.py:29
  213.9 0.1 copy.11
  214.1 0.2 multiply_reduce_fusion
  214.3 0.0 copy-done.1
  214.3 0.1 multiply_convert_fusion
  214.4 0.0 all-gather.5.cloned.1.call-done
  214.4 3.6 %fusion = bf16[1,256,4096]{2,1,0:T(8,128)(2,1)} fusion(bf16[256,256]{0,1:T(8,128)(2,1)S(1)} %bitcast.39, bf16[256,4096]{1,0:T(8,128)(2,1)} %all-gather.5.cloned.1.call-done), kind=kOutput, calls=%fused_computation.1 | convolution fusion | flops 537919488 | bytes 4325376 | tf_op jit(solution)/shard_map/dot_general | solution.py:41
  (3 shorter events, 0.0 us)
Async XLA Ops:
  6.5 85.8 %copy-start = (bf16[1,256,4096]{2,1,0:T(8,128)(2,1)S(1)}, bf16[1,256,4096]{2,1,0:T(8,128)(2,1)}, u32[]{:S(2)}) copy-start(bf16[1,256,4096]{2,1,0:T(8,128)(2,1)} %param.4) | copy-start | bytes 6291460
  6.5 85.8 %all-gather.3.cloned.1.call-start = ((), (), s32[]{:S(2)}) async-start(), calls=%async_computation.1 | async-start | bytes 6684672 | tf_op jit(solution)/shard_map/all_gather | solution.py:16
  99.4 111.7 %all-to-all-start = ((bf16[32,1,2,128,128]{4,3,2,1,0:T(8,128)(2,1)}), bf16[32,1,2,128,128]{4,3,2,1,0:T(8,128)(2,1)}, u32[]{:S(2)}, u32[]{:S(2)}) async-start(bf16[32,1,2,128,128]{4,3,2,1,0:T(8,128)(2,1)} %stack.2), calls=%async_computation | async-start | bytes 4194304 | tf_op jit(solution)/shard_map/all_to_all | solution.py:23
  112.4 101.8 %copy-start.1 = (f32[256]{0:T(256)S(1)}, f32[256]{0:T(256)}, u32[]{:S(2)}) copy-start(f32[256]{0:T(256)} %param.6) | copy-start | bytes 3076
  112.4 102.0 %all-gather.5.cloned.1.call-start = ((), (), s32[]{:S(2)}) async-start(), calls=%async_computation.2 | async-start | bytes 2228224 | tf_op jit(solution)/shard_map/all_gather | solution.py:42
Sparse Core Ops, SparseCore 0:
  10.4 81.9 all-gather.2
  116.3 61.0 all-gather.4
